TPU v7x, 512 devices: a whole 4x8x8 slice. The times are simulated.
512 devices in a mesh: rows: 64 (over y, x, core), rhs: 8 (over z).
Axes of the slice: x: 4, y: 8, z: 8, core: 2. Of those that a mesh axis runs over, the one named last changes fastest.
Arguments:
- right_side: float32 [64, 32768], P('rhs', 'rows'), may hold values from -6 to 6
- tiles: float32 [512, 7, 64, 64], P('rows'), may hold values from -2 to 5.5, as said below
- pivots: float32 [512, 64, 64], P('rows'), may hold values from -0.05 to 0.8, as said below
- columns: int32 [512, 7], P('rows'), may hold values from 0 to 511, as said below
Outputs:
- solution: float32 [64, 32768], P('rhs', 'rows')
- residual: float32 [64, 32768], P('rhs', 'rows')
Inputs may be any that keep to these rules, and one draw needn't show every extreme that they name: columns[i, 0] = i. The other six columns of block row i are i - o and i + o for three offsets o shared by all block rows, the largest of them exactly 8, in an order of the slots drawn for each block row; a column that would fall outside 0 to 511 is i itself. tiles[i, 0] is the diagonal tile of block row i; A is symmetric positive definite: the tile of block row i in a slot whose column j differs from i is the transpose of the tile of block row j in its slot whose column is i. Every pivots[i] is symmetric positive definite.
All inputs are finite; a program needn't handle non-finite values.
Results may differ from a plain program's by a relative error of at most 0.0003.
Values sent between devices are 32-bit elements; how exact they have to be, the bound alone decides.
A program may use at most 64 MiB of HBM per device.

v0:
```python
import jax
import jax.numpy as jnp
from jax import lax
from jax.sharding import PartitionSpec as P

SPAN = 8
ITERS = 2


def passed_along(value, axis, steps):
    count = lax.axis_size(axis)
    first, last = (max(0, -steps), min(count, count - steps))
    return lax.ppermute(value, axis, [(source, source + steps) for source in range(first, last)])


def extended_2(block, sides, width):
    for axis, dim in sides:
        count = lax.axis_size(axis)
        forward = [(i, i + 1) for i in range(count - 1)]
        backward = [(target, source) for source, target in forward]
        low = lax.ppermute(
            lax.slice_in_dim(block, block.shape[dim] - width, None, axis=dim), axis, forward
        )
        high = lax.ppermute(lax.slice_in_dim(block, 0, width, axis=dim), axis, backward)
        block = jnp.concatenate([low, block, high], axis=dim)
    return block


def inner(left, right):
    return jnp.dot(left, right.T, precision=lax.Precision.HIGHEST)


def chol_solve(factor, values):
    middle = lax.linalg.triangular_solve(factor, values, left_side=True, lower=True)
    return lax.linalg.triangular_solve(factor, middle, left_side=True, lower=True, transpose_a=True)


def shards(right_side, tiles, pivots, columns):
    count = right_side.shape[0]
    shard_rows = tiles.shape[0]
    width = tiles.shape[2]
    cells = shard_rows * width
    where_row = lax.axis_index("rows")
    start = where_row * shard_rows
    position = where_row % SPAN
    block_low = (where_row - position) * shard_rows
    block_high = block_low + SPAN * shard_rows
    global_rows = start + jnp.arange(shard_rows, dtype=jnp.int32)
    lower = (columns < global_rows[:, None]) & (columns >= block_low)
    upper = (columns > global_rows[:, None]) & (columns < block_high)
    lower_tiles = tiles * lower[:, :, None, None].astype(tiles.dtype)
    upper_tiles = tiles * upper[:, :, None, None].astype(tiles.dtype)
    forward_cols = jnp.clip(columns - start + shard_rows, 0, 2 * shard_rows - 1)
    backward_cols = jnp.clip(columns - start, 0, 2 * shard_rows - 1)
    halo_cols = columns - start + shard_rows
    from_below = (position != 0).astype(jnp.float32)
    from_above = (position != SPAN - 1).astype(jnp.float32)

    def forward_local(source, incoming):
        extended = jnp.concatenate([incoming, jnp.zeros_like(source)], axis=1)

        def forward_one_row(row, extended):
            picked = jnp.take(extended, forward_cols[row], axis=1)
            summed = jnp.einsum(
                "kab,ckb->ca", lower_tiles[row], picked, precision=lax.Precision.HIGHEST
            )
            remain = source[:, row] - summed
            value = jnp.einsum("ab,cb->ca", pivots[row], remain, precision=lax.Precision.HIGHEST)
            return lax.dynamic_update_slice_in_dim(extended, value[:, None], shard_rows + row, 1)

        extended = lax.fori_loop(0, shard_rows, forward_one_row, extended)
        return extended[:, shard_rows:]

    def backward_local(source, incoming):
        extended = jnp.concatenate([jnp.zeros_like(source), incoming], axis=1)

        def backward_one_row(turn, extended):
            row = shard_rows - 1 - turn
            picked = jnp.take(extended, backward_cols[row], axis=1)
            summed = jnp.einsum(
                "kab,ckb->ca", upper_tiles[row], picked, precision=lax.Precision.HIGHEST
            )
            value = source[:, row] - jnp.einsum(
                "ab,cb->ca", pivots[row], summed, precision=lax.Precision.HIGHEST
            )
            return lax.dynamic_update_slice_in_dim(extended, value[:, None], row, 1)

        extended = lax.fori_loop(0, shard_rows, backward_one_row, extended)
        return extended[:, :shard_rows]

    def precondition(vector):
        source = vector.reshape(count, shard_rows, width)
        lowered = forward_local(source, jnp.zeros_like(source))
        for turn in range(SPAN - 1):
            incoming = passed_along(lowered, "rows", 1) * from_below
            lowered = forward_local(source, incoming)
        result = backward_local(lowered, jnp.zeros_like(lowered))
        for turn in range(SPAN - 1):
            incoming = passed_along(result, "rows", -1) * from_above
            result = backward_local(lowered, incoming)
        return result.reshape(count, cells)

    solution = jnp.zeros_like(right_side)
    residual = right_side
    direction = precondition(residual)
    for turn in range(ITERS):
        blocks = extended_2(direction, (("rows", 1),), cells).reshape(count, 3 * shard_rows, width)
        apply_picked = jnp.take(blocks, halo_cols, axis=1)
        image = jnp.einsum(
            "ikab,cikb->cia", tiles, apply_picked, precision=lax.Precision.HIGHEST
        ).reshape(count, cells)
        every_direction = lax.all_gather(direction, "rhs", axis=0, tiled=True)
        partial_pq = inner(every_direction, image)
        partial_pr = inner(every_direction, residual)
        summed_pq, summed_pr = lax.psum((partial_pq, partial_pr), "rows")
        gram = lax.all_gather(summed_pq, "rhs", axis=1, tiled=True)
        factor = jnp.linalg.cholesky(0.5 * (gram + gram.T))
        alpha = chol_solve(factor, summed_pr)
        change = jnp.dot(alpha.T, every_direction, precision=lax.Precision.HIGHEST)
        solution = solution + change
        if turn + 1 < ITERS:
            every_image = lax.all_gather(image, "rhs", axis=0, tiled=True)
            residual = residual - jnp.dot(alpha.T, every_image, precision=lax.Precision.HIGHEST)
            preconditioned = precondition(residual)
            summed_qz = lax.psum(inner(every_image, preconditioned), "rows")
            beta = -chol_solve(factor, summed_qz)
            direction = preconditioned + jnp.dot(
                beta.T, every_direction, precision=lax.Precision.HIGHEST
            )
        else:
            every_image = lax.all_gather(image, "rhs", axis=0, tiled=True)
            residual = residual - jnp.dot(alpha.T, every_image, precision=lax.Precision.HIGHEST)
    return (solution, residual)


def solution(mesh):
    return jax.shard_map(
        shards,
        mesh=mesh,
        in_specs=(
            P("rhs", "rows"),
            P("rows", None, None, None),
            P("rows", None, None),
            P("rows", None),
        ),
        out_specs=(P("rhs", "rows"), P("rhs", "rows")),
        check_vma=False,
    )
```

profile of v0, /device:TPU:32, one launch (start us, length us, event | category | flops | bytes accessed | tf_op | source)
XLA Modules:
  0.0 1239.9 jit_solution(11222102633937518841)
XLA Ops:
  6.0 16.7 %while.480 = (s32[]{:T(128)}, f32[8,16,64]{2,0,1:T(8,128)S(1)}, f32[8,8,64]{2,0,1:T(8,128)S(1)}, s32[8,7]{1,0:T(8,128)S(1)}, f32[8,7,64,64]{3,2,1,0:T(8,128)}, /...) while((s32[]{:T(128)}, f32[8,16,64]{2,0,1:T(8,128)S(1)}, ...), condition=%wide.region_1.3_spmd, body=%wide.region_0.2_spmd.sunk | while | flops 3150896 | bytes 322845 | solution.py:71
  31.3 16.7 %while.481 = (s32[]{:T(128)}, f32[8,16,64]{2,0,1:T(8,128)S(1)}, f32[8,8,64]{2,0,1:T(8,128)S(1)}, s32[8,7]{1,0:T(8,128)S(1)}, f32[8,7,64,64]{3,2,1,0:T(8,128)}, /...) while((s32[]{:T(128)}, f32[8,16,64]{2,0,1:T(8,128)S(1)}, ...), condition=%wide.region_3.5_spmd, body=%wide.region_2.4_spmd.sunk | while | flops 3150896 | bytes 322845 | solution.py:71
  56.6 16.7 %while.482 = (s32[]{:T(128)}, f32[8,16,64]{2,0,1:T(8,128)S(1)}, f32[8,8,64]{2,0,1:T(8,128)S(1)}, s32[8,7]{1,0:T(8,128)S(1)}, f32[8,7,64,64]{3,2,1,0:T(8,128)}, /...) while((s32[]{:T(128)}, f32[8,16,64]{2,0,1:T(8,128)S(1)}, ...), condition=%wide.region_5.7_spmd, body=%wide.region_4.6_spmd.sunk | while | flops 3150896 | bytes 322845 | solution.py:71
  81.9 16.7 %while.483 = (s32[]{:T(128)}, f32[8,16,64]{2,0,1:T(8,128)S(1)}, f32[8,8,64]{2,0,1:T(8,128)S(1)}, s32[8,7]{1,0:T(8,128)S(1)}, f32[8,7,64,64]{3,2,1,0:T(8,128)}, /...) while((s32[]{:T(128)}, f32[8,16,64]{2,0,1:T(8,128)S(1)}, ...), condition=%wide.region_7.9_spmd, body=%wide.region_6.8_spmd.sunk | while | flops 3150896 | bytes 322845 | solution.py:71
  107.2 16.7 %while.484 = (s32[]{:T(128)}, f32[8,16,64]{2,0,1:T(8,128)S(1)}, f32[8,8,64]{2,0,1:T(8,128)S(1)}, s32[8,7]{1,0:T(8,128)S(1)}, f32[8,7,64,64]{3,2,1,0:T(8,128)}, /...) while((s32[]{:T(128)}, f32[8,16,64]{2,0,1:T(8,128)S(1)}, ...), condition=%wide.region_9.11_spmd, body=%wide.region_8.10_spmd.sunk | while | flops 3150896 | bytes 322845 | solution.py:71
  132.5 16.7 %while.485 = (s32[]{:T(128)}, f32[8,16,64]{2,0,1:T(8,128)S(1)}, f32[8,8,64]{2,0,1:T(8,128)S(1)}, s32[8,7]{1,0:T(8,128)S(1)}, f32[8,7,64,64]{3,2,1,0:T(8,128)}, /...) while((s32[]{:T(128)}, f32[8,16,64]{2,0,1:T(8,128)S(1)}, ...), condition=%wide.region_11.13_spmd, body=%wide.region_10.12_spmd.sunk | while | flops 3150896 | bytes 322845 | solution.py:71
  157.8 16.7 %while.486 = (s32[]{:T(128)}, f32[8,16,64]{2,0,1:T(8,128)S(1)}, f32[8,8,64]{2,0,1:T(8,128)S(1)}, s32[8,7]{1,0:T(8,128)S(1)}, f32[8,7,64,64]{3,2,1,0:T(8,128)}, /...) while((s32[]{:T(128)}, f32[8,16,64]{2,0,1:T(8,128)S(1)}, ...), condition=%wide.region_13.15_spmd, body=%wide.region_12.14_spmd.sunk | while | flops 3150896 | bytes 322845 | solution.py:71
  183.1 16.7 %while.487 = (s32[]{:T(128)}, f32[8,16,64]{2,0,1:T(8,128)S(1)}, f32[8,8,64]{2,0,1:T(8,128)S(1)}, s32[8,7]{1,0:T(8,128)S(1)}, f32[8,7,64,64]{3,2,1,0:T(8,128)}, /...) while((s32[]{:T(128)}, f32[8,16,64]{2,0,1:T(8,128)S(1)}, ...), condition=%wide.region_15.17_spmd, body=%wide.region_14.16_spmd.sunk | while | flops 3150896 | bytes 322845 | solution.py:71
  199.9 9.2 while.488
  230.4 9.2 while.490
  248.2 9.2 while.491
  266.0 9.2 while.492
  283.8 9.2 while.493
  301.6 9.2 while.494
  319.4 9.2 while.495
  337.6 30.9 %all_gather.18 = f32[64,512]{1,0:T(8,128)S(1)} all-gather(f32[8,512]{1,0:T(8,128)S(1)} %reshape.66), channel_id=1, replica_groups=mesh['rows'=64,'rhs'=8] {'rhs'}, dimensions={0}, use_global_device_ids=true | all-gather | bytes 147456 | tf_op jit(solution)/shard_map/all_gather | solution.py:112
  373.2 24.6 %all_gather.20 = f32[64,512]{1,0:T(8,128)S(1)} all-gather(f32[8,512]{1,0:T(8,128)S(1)} %reshape.67), channel_id=1, replica_groups=mesh['rows'=64,'rhs'=8] {'rhs'}, dimensions={0}, use_global_device_ids=true | all-gather | bytes 147456 | tf_op jit(solution)/shard_map/all_gather | solution.py:122
  397.8 126.1 %all-reduce.29 = (f32[64,8]{0,1:T(8,128)S(1)}, f32[64,8]{0,1:T(8,128)S(1)}) all-reduce(f32[64,8]{0,1:T(8,128)S(1)} %fusion.476, f32[64,8]{0,1:T(8,128)S(1)} %fusion.475), channel_id=1, replica_groups=mesh['rows'=64,'rhs'=8] {'rows'}, use_global_device_ids=true, to_apply=%region_35.39 | all-reduce | flops 1024 | bytes 8192 | tf_op jit(solution)/shard_map/psum | solution.py:115
  523.9 24.5 %all_gather.19 = f32[64,64]{0,1:T(8,128)S(1)} all-gather(f32[64,8]{0,1:T(8,128)S(1)} %get-tuple-element.5610), channel_id=1, replica_groups=mesh['rows'=64,'rhs'=8] {'rhs'}, dimensions={1}, use_global_device_ids=true | all-gather | bytes 18432 | tf_op jit(solution)/shard_map/all_gather | solution.py:116
  561.3 16.7 %while.496 = (s32[]{:T(128)}, f32[8,16,64]{2,0,1:T(8,128)S(1)}, f32[8,8,64]{2,0,1:T(8,128)S(1)}, s32[8,7]{1,0:T(8,128)S(1)}, f32[8,7,64,64]{3,2,1,0:T(8,128)}, /...) while((s32[]{:T(128)}, f32[8,16,64]{2,0,1:T(8,128)S(1)}, ...), condition=%wide.region_37.43_spmd, body=%wide.region_36.42_spmd.sunk | while | flops 3150896 | bytes 322845 | solution.py:71
  586.6 16.7 %while.497 = (s32[]{:T(128)}, f32[8,16,64]{2,0,1:T(8,128)S(1)}, f32[8,8,64]{2,0,1:T(8,128)S(1)}, s32[8,7]{1,0:T(8,128)S(1)}, f32[8,7,64,64]{3,2,1,0:T(8,128)}, /...) while((s32[]{:T(128)}, f32[8,16,64]{2,0,1:T(8,128)S(1)}, ...), condition=%wide.region_39.45_spmd, body=%wide.region_38.44_spmd.sunk | while | flops 3150896 | bytes 322845 | solution.py:71
  611.9 16.7 %while.498 = (s32[]{:T(128)}, f32[8,16,64]{2,0,1:T(8,128)S(1)}, f32[8,8,64]{2,0,1:T(8,128)S(1)}, s32[8,7]{1,0:T(8,128)S(1)}, f32[8,7,64,64]{3,2,1,0:T(8,128)}, /...) while((s32[]{:T(128)}, f32[8,16,64]{2,0,1:T(8,128)S(1)}, ...), condition=%wide.region_41.47_spmd, body=%wide.region_40.46_spmd.sunk | while | flops 3150896 | bytes 322845 | solution.py:71
  637.2 16.7 %while.499 = (s32[]{:T(128)}, f32[8,16,64]{2,0,1:T(8,128)S(1)}, f32[8,8,64]{2,0,1:T(8,128)S(1)}, s32[8,7]{1,0:T(8,128)S(1)}, f32[8,7,64,64]{3,2,1,0:T(8,128)}, /...) while((s32[]{:T(128)}, f32[8,16,64]{2,0,1:T(8,128)S(1)}, ...), condition=%wide.region_43.49_spmd, body=%wide.region_42.48_spmd.sunk | while | flops 3150896 | bytes 322845 | solution.py:71
  662.5 16.7 %while.500 = (s32[]{:T(128)}, f32[8,16,64]{2,0,1:T(8,128)S(1)}, f32[8,8,64]{2,0,1:T(8,128)S(1)}, s32[8,7]{1,0:T(8,128)S(1)}, f32[8,7,64,64]{3,2,1,0:T(8,128)}, /...) while((s32[]{:T(128)}, f32[8,16,64]{2,0,1:T(8,128)S(1)}, ...), condition=%wide.region_45.51_spmd, body=%wide.region_44.50_spmd.sunk | while | flops 3150896 | bytes 322845 | solution.py:71
  687.8 16.7 %while.501 = (s32[]{:T(128)}, f32[8,16,64]{2,0,1:T(8,128)S(1)}, f32[8,8,64]{2,0,1:T(8,128)S(1)}, s32[8,7]{1,0:T(8,128)S(1)}, f32[8,7,64,64]{3,2,1,0:T(8,128)}, /...) while((s32[]{:T(128)}, f32[8,16,64]{2,0,1:T(8,128)S(1)}, ...), condition=%wide.region_47.53_spmd, body=%wide.region_46.52_spmd.sunk | while | flops 3150896 | bytes 322845 | solution.py:71
  713.1 16.7 %while.502 = (s32[]{:T(128)}, f32[8,16,64]{2,0,1:T(8,128)S(1)}, f32[8,8,64]{2,0,1:T(8,128)S(1)}, s32[8,7]{1,0:T(8,128)S(1)}, f32[8,7,64,64]{3,2,1,0:T(8,128)}, /...) while((s32[]{:T(128)}, f32[8,16,64]{2,0,1:T(8,128)S(1)}, ...), condition=%wide.region_49.55_spmd, body=%wide.region_48.54_spmd.sunk | while | flops 3150896 | bytes 322845 | solution.py:71
  738.4 16.7 %while.503 = (s32[]{:T(128)}, f32[8,16,64]{2,0,1:T(8,128)S(1)}, f32[8,8,64]{2,0,1:T(8,128)S(1)}, s32[8,7]{1,0:T(8,128)S(1)}, f32[8,7,64,64]{3,2,1,0:T(8,128)}, /...) while((s32[]{:T(128)}, f32[8,16,64]{2,0,1:T(8,128)S(1)}, ...), condition=%wide.region_51.57_spmd, body=%wide.region_50.56_spmd.sunk | while | flops 3150896 | bytes 322845 | solution.py:71
  884.2 129.3 %psum.37 = f32[64,8]{0,1:T(8,128)S(1)} all-reduce(f32[64,8]{0,1:T(8,128)S(1)} %fusion.478), channel_id=1, replica_groups=mesh['rows'=64,'rhs'=8] {'rows'}, use_global_device_ids=true, to_apply=%region_68.74 | all-reduce | flops 512 | bytes 4096 | tf_op jit(solution)/shard_map/psum | solution.py:125
  1022.8 24.6 %all_gather.21 = f32[64,512]{1,0:T(8,128)S(1)} all-gather(f32[8,512]{1,0:T(8,128)S(1)} %convolution_add_fusion.1), channel_id=1, replica_groups=mesh['rows'=64,'rhs'=8] {'rhs'}, dimensions={0}, use_global_device_ids=true | all-gather | bytes 147456 | tf_op jit(solution)/shard_map/all_gather | solution.py:112
  1050.5 24.6 %all_gather.23 = f32[64,512]{1,0:T(8,128)S(1)} all-gather(f32[8,512]{1,0:T(8,128)S(1)} %reshape.71), channel_id=1, replica_groups=mesh['rows'=64,'rhs'=8] {'rhs'}, dimensions={0}, use_global_device_ids=true | all-gather | bytes 147456 | tf_op jit(solution)/shard_map/all_gather | solution.py:131
  1075.2 126.1 %all-reduce.28 = (f32[64,8]{0,1:T(8,128)S(1)}, f32[64,8]{0,1:T(8,128)S(1)}) all-reduce(f32[64,8]{0,1:T(8,128)S(1)} %fusion.480, f32[64,8]{0,1:T(8,128)S(1)} %fusion.479), channel_id=1, replica_groups=mesh['rows'=64,'rhs'=8] {'rows'}, use_global_device_ids=true, to_apply=%region_70.76 | all-reduce | flops 1024 | bytes 8192 | tf_op jit(solution)/shard_map/psum | solution.py:115
  1201.3 24.5 %all_gather.22 = f32[64,64]{0,1:T(8,128)S(1)} all-gather(f32[64,8]{0,1:T(8,128)S(1)} %get-tuple-element.5608), channel_id=1, replica_groups=mesh['rows'=64,'rhs'=8] {'rhs'}, dimensions={1}, use_global_device_ids=true | all-gather | bytes 18432 | tf_op jit(solution)/shard_map/all_gather | solution.py:116
  (1515 shorter events, 779.3 us)
Async XLA Ops:
  22.7 8.6 collective-permute-start
  48.0 8.6 collective-permute-start.1
  73.3 8.6 collective-permute-start.2
  98.6 8.6 collective-permute-start.3
  123.9 8.6 collective-permute-start.4
  149.2 8.6 collective-permute-start.5
  174.5 8.6 collective-permute-start.6
  209.1 3.5 collective-permute-start.7
  221.8 8.6 collective-permute-start.8
  239.6 8.6 collective-permute-start.9
  257.4 8.6 collective-permute-start.10
  275.2 8.6 collective-permute-start.11
  293.0 8.6 collective-permute-start.12
  310.8 8.6 collective-permute-start.13
  328.7 40.0 %collective-permute-start.14 = (f32[8,512]{1,0:T(8,128)S(1)}, f32[8,512]{1,0:T(8,128)S(1)}, u32[]{:S(2)}, u32[]{:S(2)}) collective-permute-start(f32[8,512]{1,0:T(8,128)S(1)} %reshape.66), channel_id=1, source_target_pairs={{0,8},{8,16},{16,24},{24,32},{32,40},{40,48},{48,56},{56,64},{64,7... | collective-permute-start | bytes 49160 | tf_op jit(solution)/shard_map/ppermute | solution.py:21
  330.6 38.2 %collective-permute-start.15 = (f32[8,512]{1,0:T(8,128)S(1)}, f32[8,512]{1,0:T(8,128)S(1)}, u32[]{:S(2)}, u32[]{:S(2)}) collective-permute-start(f32[8,512]{1,0:T(8,128)S(1)} %reshape.66), channel_id=1, source_target_pairs={{8,0},{16,8},{24,16},{32,24},{40,32},{48,40},{56,48},{64,56},{72,6... | collective-permute-start | bytes 49160 | tf_op jit(solution)/shard_map/ppermute | solution.py:24
  578.0 8.6 collective-permute-start.16
  603.3 8.6 collective-permute-start.17
  628.6 8.6 collective-permute-start.18
  653.9 8.6 collective-permute-start.19
  679.2 8.6 collective-permute-start.20
  704.5 8.6 collective-permute-start.21
  729.8 8.6 collective-permute-start.22
  764.4 3.5 collective-permute-start.23
  777.1 8.6 collective-permute-start.24
  794.9 8.6 collective-permute-start.25
  812.7 8.6 collective-permute-start.26
  830.5 8.6 collective-permute-start.27
  848.3 8.6 collective-permute-start.28
  866.1 8.6 collective-permute-start.29
  1013.9 33.6 %collective-permute-start.30 = (f32[8,512]{1,0:T(8,128)S(1)}, f32[8,512]{1,0:T(8,128)S(1)}, u32[]{:S(2)}, u32[]{:S(2)}) collective-permute-start(f32[8,512]{1,0:T(8,128)S(1)} %convolution_add_fusion.1), channel_id=1, source_target_pairs={{0,8},{8,16},{16,24},{24,32},{32,40},{40,48},{48,56},{56,64},{64,7... | collective-permute-start | bytes 49160 | tf_op jit(solution)/shard_map/ppermute | solution.py:21
  1015.9 31.8 %collective-permute-start.31 = (f32[8,512]{1,0:T(8,128)S(1)}, f32[8,512]{1,0:T(8,128)S(1)}, u32[]{:S(2)}, u32[]{:S(2)}) collective-permute-start(f32[8,512]{1,0:T(8,128)S(1)} %convolution_add_fusion.1), channel_id=1, source_target_pairs={{8,0},{16,8},{24,16},{32,24},{40,32},{48,40},{56,48},{64,56},{72,6... | collective-permute-start | bytes 49160 | tf_op jit(solution)/shard_map/ppermute | solution.py:24
  (3 other events, 225.4 us)
where the time goes:
time: 1240 us
  blocking collectives  535 us (43%)
  matrix products  265 us (21%)
  local copies, waits for them, and re-layouts  146 us (12%)
  starting transfers between devices  133 us (11%)
  waiting for transfers between devices  114 us (9%)
  other arithmetic  39.3 us (3%)
    psum x2, blocking collectives, shards(): summed_pq, summed_pr = lax.psum((partial_pq, partial_pr), 'rows')  252 us
    dot_general x128, matrix products, forward_one_row(): jnp.einsum('kab,ckb->ca', lower_tiles[row], picked, precision=lax.Precisi...  162 us
    psum x1, blocking collectives, shards(): summed_qz = lax.psum(inner(every_image, preconditioned), 'rows')  129 us
    ppermute x28, starting transfers between devices, passed_along(): lax.ppermute(value, axis, [(source, source + steps) for source in range(f...  115 us
    ppermute x28, waiting for transfers between devices, passed_along(): lax.ppermute(value, axis, [(source, source + steps) for source in range(f...  114 us
    gather x128, local copies, waits for them, and re-layouts, forward_one_row(): picked = jnp.take(extended, forward_cols[row], axis=1)  70.9 us
    gather x128, local copies, waits for them, and re-layouts, backward_one_row(): picked = jnp.take(extended, backward_cols[row], axis=1)  70.9 us
    all_gather x2, blocking collectives, shards(): every_direction = lax.all_gather(direction, 'rhs', axis=0, tiled=True)  55.5 us
  transfers between devices with their start and end apart: 32, of which 28 were waited for; matrix products, arithmetic and copies ran while one was open for 0% of the time, Pallas kernels for 0%

commit v1 on v0

--- a/solution.py
+++ b/solution.py
@@ -122,7 +122,7 @@
             every_image = lax.all_gather(image, "rhs", axis=0, tiled=True)
             residual = residual - jnp.dot(alpha.T, every_image, precision=lax.Precision.HIGHEST)
             preconditioned = precondition(residual)
-            summed_qz = lax.psum(inner(every_image, preconditioned), "rows")
+            summed_qz = jnp.sum(lax.all_gather(inner(every_image, preconditioned), "rows"), axis=0)
             beta = -chol_solve(factor, summed_qz)
             direction = preconditioned + jnp.dot(
                 beta.T, every_direction, precision=lax.Precision.HIGHEST

time: 1240 us -> 1150 us (0.927)
  blocking collectives: 535 us -> 443 us
    psum x1 -> x0, blocking collectives: 129 us -> none  [shards(): summed_qz = lax.psum(inner(every_image, preconditioned), 'rows')]
    all_gather x0 -> x1, blocking collectives: none -> 37.4 us  [shards(): lax.all_gather(inner(every_image, preconditioned), 'rows')]
where the time goes in v1:
time: 1150 us
  blocking collectives  443 us (39%)
  matrix products  265 us (23%)
  local copies, waits for them, and re-layouts  146 us (13%)
  starting transfers between devices  133 us (12%)
  waiting for transfers between devices  114 us (10%)
  other arithmetic  39.3 us (3%)
    psum x2, blocking collectives, shards(): summed_pq, summed_pr = lax.psum((partial_pq, partial_pr), 'rows')  252 us
    dot_general x128, matrix products, forward_one_row(): jnp.einsum('kab,ckb->ca', lower_tiles[row], picked, precision=lax.Precisi...  162 us
    ppermute x28, starting transfers between devices, passed_along(): lax.ppermute(value, axis, [(source, source + steps) for source in range(f...  115 us
    ppermute x28, waiting for transfers between devices, passed_along(): lax.ppermute(value, axis, [(source, source + steps) for source in range(f...  114 us
    gather x128, local copies, waits for them, and re-layouts, forward_one_row(): picked = jnp.take(extended, forward_cols[row], axis=1)  70.9 us
    gather x128, local copies, waits for them, and re-layouts, backward_one_row(): picked = jnp.take(extended, backward_cols[row], axis=1)  70.9 us
    all_gather x2, blocking collectives, shards(): every_direction = lax.all_gather(direction, 'rhs', axis=0, tiled=True)  55.5 us
    all_gather x2, blocking collectives, shards(): every_image = lax.all_gather(image, 'rhs', axis=0, tiled=True)  49.2 us
  transfers between devices with their start and end apart: 32, of which 28 were waited for; matrix products, arithmetic and copies ran while one was open for 0% of the time, Pallas kernels for 0%

profile of v1, /device:TPU:32, one launch (start us, length us, event | category | flops | bytes accessed | tf_op | source)
XLA Modules:
  0.0 1148.1 jit_solution(8598031179956018081)
XLA Ops:
  6.0 16.7 %while.480 = (s32[]{:T(128)}, f32[8,16,64]{2,0,1:T(8,128)S(1)}, f32[8,8,64]{2,0,1:T(8,128)S(1)}, s32[8,7]{1,0:T(8,128)S(1)}, f32[8,7,64,64]{3,2,1,0:T(8,128)}, /...) while((s32[]{:T(128)}, f32[8,16,64]{2,0,1:T(8,128)S(1)}, ...), condition=%wide.region_1.3_spmd, body=%wide.region_0.2_spmd.sunk | while | flops 3150896 | bytes 322845 | solution.py:71
  31.3 16.7 %while.481 = (s32[]{:T(128)}, f32[8,16,64]{2,0,1:T(8,128)S(1)}, f32[8,8,64]{2,0,1:T(8,128)S(1)}, s32[8,7]{1,0:T(8,128)S(1)}, f32[8,7,64,64]{3,2,1,0:T(8,128)}, /...) while((s32[]{:T(128)}, f32[8,16,64]{2,0,1:T(8,128)S(1)}, ...), condition=%wide.region_3.5_spmd, body=%wide.region_2.4_spmd.sunk | while | flops 3150896 | bytes 322845 | solution.py:71
  56.6 16.7 %while.482 = (s32[]{:T(128)}, f32[8,16,64]{2,0,1:T(8,128)S(1)}, f32[8,8,64]{2,0,1:T(8,128)S(1)}, s32[8,7]{1,0:T(8,128)S(1)}, f32[8,7,64,64]{3,2,1,0:T(8,128)}, /...) while((s32[]{:T(128)}, f32[8,16,64]{2,0,1:T(8,128)S(1)}, ...), condition=%wide.region_5.7_spmd, body=%wide.region_4.6_spmd.sunk | while | flops 3150896 | bytes 322845 | solution.py:71
  81.9 16.7 %while.483 = (s32[]{:T(128)}, f32[8,16,64]{2,0,1:T(8,128)S(1)}, f32[8,8,64]{2,0,1:T(8,128)S(1)}, s32[8,7]{1,0:T(8,128)S(1)}, f32[8,7,64,64]{3,2,1,0:T(8,128)}, /...) while((s32[]{:T(128)}, f32[8,16,64]{2,0,1:T(8,128)S(1)}, ...), condition=%wide.region_7.9_spmd, body=%wide.region_6.8_spmd.sunk | while | flops 3150896 | bytes 322845 | solution.py:71
  107.2 16.7 %while.484 = (s32[]{:T(128)}, f32[8,16,64]{2,0,1:T(8,128)S(1)}, f32[8,8,64]{2,0,1:T(8,128)S(1)}, s32[8,7]{1,0:T(8,128)S(1)}, f32[8,7,64,64]{3,2,1,0:T(8,128)}, /...) while((s32[]{:T(128)}, f32[8,16,64]{2,0,1:T(8,128)S(1)}, ...), condition=%wide.region_9.11_spmd, body=%wide.region_8.10_spmd.sunk | while | flops 3150896 | bytes 322845 | solution.py:71
  132.5 16.7 %while.485 = (s32[]{:T(128)}, f32[8,16,64]{2,0,1:T(8,128)S(1)}, f32[8,8,64]{2,0,1:T(8,128)S(1)}, s32[8,7]{1,0:T(8,128)S(1)}, f32[8,7,64,64]{3,2,1,0:T(8,128)}, /...) while((s32[]{:T(128)}, f32[8,16,64]{2,0,1:T(8,128)S(1)}, ...), condition=%wide.region_11.13_spmd, body=%wide.region_10.12_spmd.sunk | while | flops 3150896 | bytes 322845 | solution.py:71
  157.8 16.7 %while.486 = (s32[]{:T(128)}, f32[8,16,64]{2,0,1:T(8,128)S(1)}, f32[8,8,64]{2,0,1:T(8,128)S(1)}, s32[8,7]{1,0:T(8,128)S(1)}, f32[8,7,64,64]{3,2,1,0:T(8,128)}, /...) while((s32[]{:T(128)}, f32[8,16,64]{2,0,1:T(8,128)S(1)}, ...), condition=%wide.region_13.15_spmd, body=%wide.region_12.14_spmd.sunk | while | flops 3150896 | bytes 322845 | solution.py:71
  183.1 16.7 %while.487 = (s32[]{:T(128)}, f32[8,16,64]{2,0,1:T(8,128)S(1)}, f32[8,8,64]{2,0,1:T(8,128)S(1)}, s32[8,7]{1,0:T(8,128)S(1)}, f32[8,7,64,64]{3,2,1,0:T(8,128)}, /...) while((s32[]{:T(128)}, f32[8,16,64]{2,0,1:T(8,128)S(1)}, ...), condition=%wide.region_15.17_spmd, body=%wide.region_14.16_spmd.sunk | while | flops 3150896 | bytes 322845 | solution.py:71
  199.9 9.2 while.488
  230.4 9.2 while.490
  248.2 9.2 while.491
  266.0 9.2 while.492
  283.8 9.2 while.493
  301.6 9.2 while.494
  319.4 9.2 while.495
  337.6 30.9 %all_gather.24 = f32[64,512]{1,0:T(8,128)S(1)} all-gather(f32[8,512]{1,0:T(8,128)S(1)} %reshape.66), channel_id=1, replica_groups=mesh['rows'=64,'rhs'=8] {'rhs'}, dimensions={0}, use_global_device_ids=true | all-gather | bytes 147456 | tf_op jit(solution)/shard_map/all_gather | solution.py:112
  373.2 24.6 %all_gather.26 = f32[64,512]{1,0:T(8,128)S(1)} all-gather(f32[8,512]{1,0:T(8,128)S(1)} %reshape.67), channel_id=1, replica_groups=mesh['rows'=64,'rhs'=8] {'rhs'}, dimensions={0}, use_global_device_ids=true | all-gather | bytes 147456 | tf_op jit(solution)/shard_map/all_gather | solution.py:122
  397.8 126.1 %all-reduce.29 = (f32[64,8]{0,1:T(8,128)S(1)}, f32[64,8]{0,1:T(8,128)S(1)}) all-reduce(f32[64,8]{0,1:T(8,128)S(1)} %fusion.476, f32[64,8]{0,1:T(8,128)S(1)} %fusion.475), channel_id=1, replica_groups=mesh['rows'=64,'rhs'=8] {'rows'}, use_global_device_ids=true, to_apply=%region_35.39 | all-reduce | flops 1024 | bytes 8192 | tf_op jit(solution)/shard_map/psum | solution.py:115
  523.9 24.5 %all_gather.25 = f32[64,64]{0,1:T(8,128)S(1)} all-gather(f32[64,8]{0,1:T(8,128)S(1)} %get-tuple-element.5610), channel_id=1, replica_groups=mesh['rows'=64,'rhs'=8] {'rhs'}, dimensions={1}, use_global_device_ids=true | all-gather | bytes 18432 | tf_op jit(solution)/shard_map/all_gather | solution.py:116
  561.3 16.7 %while.496 = (s32[]{:T(128)}, f32[8,16,64]{2,0,1:T(8,128)S(1)}, f32[8,8,64]{2,0,1:T(8,128)S(1)}, s32[8,7]{1,0:T(8,128)S(1)}, f32[8,7,64,64]{3,2,1,0:T(8,128)}, /...) while((s32[]{:T(128)}, f32[8,16,64]{2,0,1:T(8,128)S(1)}, ...), condition=%wide.region_37.43_spmd, body=%wide.region_36.42_spmd.sunk | while | flops 3150896 | bytes 322845 | solution.py:71
  586.6 16.7 %while.497 = (s32[]{:T(128)}, f32[8,16,64]{2,0,1:T(8,128)S(1)}, f32[8,8,64]{2,0,1:T(8,128)S(1)}, s32[8,7]{1,0:T(8,128)S(1)}, f32[8,7,64,64]{3,2,1,0:T(8,128)}, /...) while((s32[]{:T(128)}, f32[8,16,64]{2,0,1:T(8,128)S(1)}, ...), condition=%wide.region_39.45_spmd, body=%wide.region_38.44_spmd.sunk | while | flops 3150896 | bytes 322845 | solution.py:71
  611.9 16.7 %while.498 = (s32[]{:T(128)}, f32[8,16,64]{2,0,1:T(8,128)S(1)}, f32[8,8,64]{2,0,1:T(8,128)S(1)}, s32[8,7]{1,0:T(8,128)S(1)}, f32[8,7,64,64]{3,2,1,0:T(8,128)}, /...) while((s32[]{:T(128)}, f32[8,16,64]{2,0,1:T(8,128)S(1)}, ...), condition=%wide.region_41.47_spmd, body=%wide.region_40.46_spmd.sunk | while | flops 3150896 | bytes 322845 | solution.py:71
  637.2 16.7 %while.499 = (s32[]{:T(128)}, f32[8,16,64]{2,0,1:T(8,128)S(1)}, f32[8,8,64]{2,0,1:T(8,128)S(1)}, s32[8,7]{1,0:T(8,128)S(1)}, f32[8,7,64,64]{3,2,1,0:T(8,128)}, /...) while((s32[]{:T(128)}, f32[8,16,64]{2,0,1:T(8,128)S(1)}, ...), condition=%wide.region_43.49_spmd, body=%wide.region_42.48_spmd.sunk | while | flops 3150896 | bytes 322845 | solution.py:71
  662.5 16.7 %while.500 = (s32[]{:T(128)}, f32[8,16,64]{2,0,1:T(8,128)S(1)}, f32[8,8,64]{2,0,1:T(8,128)S(1)}, s32[8,7]{1,0:T(8,128)S(1)}, f32[8,7,64,64]{3,2,1,0:T(8,128)}, /...) while((s32[]{:T(128)}, f32[8,16,64]{2,0,1:T(8,128)S(1)}, ...), condition=%wide.region_45.51_spmd, body=%wide.region_44.50_spmd.sunk | while | flops 3150896 | bytes 322845 | solution.py:71
  687.8 16.7 %while.501 = (s32[]{:T(128)}, f32[8,16,64]{2,0,1:T(8,128)S(1)}, f32[8,8,64]{2,0,1:T(8,128)S(1)}, s32[8,7]{1,0:T(8,128)S(1)}, f32[8,7,64,64]{3,2,1,0:T(8,128)}, /...) while((s32[]{:T(128)}, f32[8,16,64]{2,0,1:T(8,128)S(1)}, ...), condition=%wide.region_47.53_spmd, body=%wide.region_46.52_spmd.sunk | while | flops 3150896 | bytes 322845 | solution.py:71
  713.1 16.7 %while.502 = (s32[]{:T(128)}, f32[8,16,64]{2,0,1:T(8,128)S(1)}, f32[8,8,64]{2,0,1:T(8,128)S(1)}, s32[8,7]{1,0:T(8,128)S(1)}, f32[8,7,64,64]{3,2,1,0:T(8,128)}, /...) while((s32[]{:T(128)}, f32[8,16,64]{2,0,1:T(8,128)S(1)}, ...), condition=%wide.region_49.55_spmd, body=%wide.region_48.54_spmd.sunk | while | flops 3150896 | bytes 322845 | solution.py:71
  738.4 16.7 %while.503 = (s32[]{:T(128)}, f32[8,16,64]{2,0,1:T(8,128)S(1)}, f32[8,8,64]{2,0,1:T(8,128)S(1)}, s32[8,7]{1,0:T(8,128)S(1)}, f32[8,7,64,64]{3,2,1,0:T(8,128)}, /...) while((s32[]{:T(128)}, f32[8,16,64]{2,0,1:T(8,128)S(1)}, ...), condition=%wide.region_51.57_spmd, body=%wide.region_50.56_spmd.sunk | while | flops 3150896 | bytes 322845 | solution.py:71
  884.2 37.4 %all-gather.1 = f32[64,64,8]{1,2,0:T(8,128)S(1)} all-gather(f32[1,64,8]{1,2,0:T(8,128)S(1)} %convolution_bitcast_fusion.50), channel_id=2, replica_groups=mesh['rows'=64,'rhs'=8] {'rows'}, dimensions={0}, use_global_device_ids=true | all-gather | bytes 133120 | tf_op jit(solution)/shard_map/all_gather | solution.py:125
  931.0 24.6 %all_gather.29 = f32[64,512]{1,0:T(8,128)S(1)} all-gather(f32[8,512]{1,0:T(8,128)S(1)} %convolution_add_fusion.1), channel_id=1, replica_groups=mesh['rows'=64,'rhs'=8] {'rhs'}, dimensions={0}, use_global_device_ids=true | all-gather | bytes 147456 | tf_op jit(solution)/shard_map/all_gather | solution.py:112
  958.7 24.6 %all_gather.31 = f32[64,512]{1,0:T(8,128)S(1)} all-gather(f32[8,512]{1,0:T(8,128)S(1)} %reshape.71), channel_id=1, replica_groups=mesh['rows'=64,'rhs'=8] {'rhs'}, dimensions={0}, use_global_device_ids=true | all-gather | bytes 147456 | tf_op jit(solution)/shard_map/all_gather | solution.py:131
  983.3 126.1 %all-reduce.28 = (f32[64,8]{0,1:T(8,128)S(1)}, f32[64,8]{0,1:T(8,128)S(1)}) all-reduce(f32[64,8]{0,1:T(8,128)S(1)} %fusion.479, f32[64,8]{0,1:T(8,128)S(1)} %fusion.478), channel_id=1, replica_groups=mesh['rows'=64,'rhs'=8] {'rows'}, use_global_device_ids=true, to_apply=%region_70.76 | all-reduce | flops 1024 | bytes 8192 | tf_op jit(solution)/shard_map/psum | solution.py:115
  1109.4 24.5 %all_gather.30 = f32[64,64]{0,1:T(8,128)S(1)} all-gather(f32[64,8]{0,1:T(8,128)S(1)} %get-tuple-element.5608), channel_id=1, replica_groups=mesh['rows'=64,'rhs'=8] {'rhs'}, dimensions={1}, use_global_device_ids=true | all-gather | bytes 18432 | tf_op jit(solution)/shard_map/all_gather | solution.py:116
  (1516 shorter events, 779.4 us)
Async XLA Ops:
  22.7 8.6 collective-permute-start
  48.0 8.6 collective-permute-start.1
  73.3 8.6 collective-permute-start.2
  98.6 8.6 collective-permute-start.3
  123.9 8.6 collective-permute-start.4
  149.2 8.6 collective-permute-start.5
  174.5 8.6 collective-permute-start.6
  209.1 3.5 collective-permute-start.7
  221.8 8.6 collective-permute-start.8
  239.6 8.6 collective-permute-start.9
  257.4 8.6 collective-permute-start.10
  275.2 8.6 collective-permute-start.11
  293.0 8.6 collective-permute-start.12
  310.8 8.6 collective-permute-start.13
  328.7 40.0 %collective-permute-start.14 = (f32[8,512]{1,0:T(8,128)S(1)}, f32[8,512]{1,0:T(8,128)S(1)}, u32[]{:S(2)}, u32[]{:S(2)}) collective-permute-start(f32[8,512]{1,0:T(8,128)S(1)} %reshape.66), channel_id=1, source_target_pairs={{0,8},{8,16},{16,24},{24,32},{32,40},{40,48},{48,56},{56,64},{64,7... | collective-permute-start | bytes 49160 | tf_op jit(solution)/shard_map/ppermute | solution.py:21
  330.6 38.2 %collective-permute-start.15 = (f32[8,512]{1,0:T(8,128)S(1)}, f32[8,512]{1,0:T(8,128)S(1)}, u32[]{:S(2)}, u32[]{:S(2)}) collective-permute-start(f32[8,512]{1,0:T(8,128)S(1)} %reshape.66), channel_id=1, source_target_pairs={{8,0},{16,8},{24,16},{32,24},{40,32},{48,40},{56,48},{64,56},{72,6... | collective-permute-start | bytes 49160 | tf_op jit(solution)/shard_map/ppermute | solution.py:24
  578.0 8.6 collective-permute-start.16
  603.3 8.6 collective-permute-start.17
  628.6 8.6 collective-permute-start.18
  653.9 8.6 collective-permute-start.19
  679.2 8.6 collective-permute-start.20
  704.5 8.6 collective-permute-start.21
  729.8 8.6 collective-permute-start.22
  764.4 3.5 collective-permute-start.23
  777.1 8.6 collective-permute-start.24
  794.9 8.6 collective-permute-start.25
  812.7 8.6 collective-permute-start.26
  830.5 8.6 collective-permute-start.27
  848.3 8.6 collective-permute-start.28
  866.1 8.6 collective-permute-start.29
  922.1 33.6 %collective-permute-start.30 = (f32[8,512]{1,0:T(8,128)S(1)}, f32[8,512]{1,0:T(8,128)S(1)}, u32[]{:S(2)}, u32[]{:S(2)}) collective-permute-start(f32[8,512]{1,0:T(8,128)S(1)} %convolution_add_fusion.1), channel_id=1, source_target_pairs={{0,8},{8,16},{16,24},{24,32},{32,40},{40,48},{48,56},{56,64},{64,7... | collective-permute-start | bytes 49160 | tf_op jit(solution)/shard_map/ppermute | solution.py:21
  924.4 31.4 %collective-permute-start.31 = (f32[8,512]{1,0:T(8,128)S(1)}, f32[8,512]{1,0:T(8,128)S(1)}, u32[]{:S(2)}, u32[]{:S(2)}) collective-permute-start(f32[8,512]{1,0:T(8,128)S(1)} %convolution_add_fusion.1), channel_id=1, source_target_pairs={{8,0},{16,8},{24,16},{32,24},{40,32},{48,40},{56,48},{64,56},{72,6... | collective-permute-start | bytes 49160 | tf_op jit(solution)/shard_map/ppermute | solution.py:24
  (3 other events, 133.5 us)
